TPU v7x, 512 devices: a whole 4x4x16 slice. The times are simulated.
512 devices in a mesh: slab: 128 (over y, z, core), sub: 4 (over x).
Axes of the slice: x: 4, y: 4, z: 16, core: 2. Of those that a mesh axis runs over, the one named last changes fastest.
Arguments:
- orbitals: float32 [256, 96, 9216], P('slab', None, 'sub'), may hold values from -6 to 6
- external_potential: float32 [1024, 12288], P('slab', 'sub'), may hold values from -6 to 6
- corners: int32 [256, 2], replicated, may hold values from 0 to 1023, as said below
- pair_list: int32 [256, 2], P('slab'), may hold values from 0 to 255, as said below
- pair_count: int32 [128], P('slab'), may hold values from 1 to 2, as said below
Outputs:
- applied_orbitals: float32 [256, 96, 9216], P('slab', None, 'sub')
Inputs may be any that keep to these rules, and one draw needn't show every extreme that they name: `corners`: column 0 is the box's first x plane: for orbital o it lies in the 32 planes that begin at plane 8 * (o // 2), taken mod 1024. Column 1 is the box's first z column (0 to 32). `pair_list`: orbital o is held by slab device o // 2. Rows 2 * d to 2 * d + 1 are the slots of slab device d; in each row (i, j), i is one of device d's orbitals, and j differs from i and is one of device d's orbitals or of device (d + 1) mod 128's. Rows that are not live hold such pairs too. `pair_count`: some slab device has 2 live slots in every draw.
All inputs are finite; a program needn't handle non-finite values.
Results may differ from a plain program's by a relative error of at most 0.0003.
Values sent between devices are 32-bit elements; how exact they have to be, the bound alone decides.
A program may use at most 64 MiB of HBM per device.

v0:
```python
import functools
import math

import jax
import jax.numpy as jnp
import ml_dtypes
import numpy as np
from jax import lax
from jax.experimental import pallas as pl
from jax.experimental.pallas import tpu as pltpu
from jax.sharding import PartitionSpec as P

SCREEN = 0.0008
FOCK_SHARE = 0.25
LOCAL_FACTOR = (3.0 / math.pi) ** (1.0 / 3.0)
EPSILON = 1e-06

B = 96
ROWS = 24
GZ = 128
SX = 8
REACH = 16
SUBS = 4
GROUP = 4
CHUNKS = ROWS // GROUP
LANES = GROUP * B
GLANES = GROUP * GZ
EDGE = 128
RING = 3
RL = ROWS * GZ // RING

F32 = jnp.float32
BF16 = jnp.bfloat16
MESH = pl.DeviceIdType.MESH


def halves(value):
    high = value.astype(ml_dtypes.bfloat16)
    low = (value - high.astype(np.float64)).astype(ml_dtypes.bfloat16)
    return high, low


def tables():
    level = np.arange(B, dtype=np.float64) + 1.0
    sine = math.sqrt(2.0 / (B + 1)) * np.sin(math.pi * level[:, None] * level[None, :] / (B + 1))
    eigen = 2.0 - 2.0 * np.cos(math.pi * level / (B + 1))
    high, low = halves(sine)
    left = np.concatenate([high, low], axis=0)
    wide = np.zeros((LANES, GLANES), np.float64)
    for k in range(GROUP):
        wide[k * B : (k + 1) * B, k * GZ : k * GZ + B] = sine
    wide_high, wide_low = halves(wide)
    narrow_high, narrow_low = wide_high.T.copy(), wide_low.T.copy()
    rows = np.arange(LANES + 2 * EDGE)[:, None] - EDGE
    cols = np.arange(LANES)[None, :]
    beside = np.abs(rows - cols)
    near = (beside == B) | ((beside == 1) & (rows // B == cols // B))
    near = near.astype(ml_dtypes.bfloat16)
    line = np.abs(np.arange(B)[:, None] - np.arange(B)[None, :])
    column = ((line == 1) * 1.0 - (line == 0) * 6.0).astype(ml_dtypes.bfloat16)
    level_bc = np.ones((B, GZ), np.float64)
    level_bc[:, :B] = eigen[:, None] + eigen[None, :] + SCREEN
    return (
        left,
        wide_high,
        wide_low,
        narrow_high,
        narrow_low,
        near,
        column,
        level_bc.astype(np.float32),
        eigen.astype(np.float32),
    )


def split(value):
    high = value.astype(BF16)
    low = (value - high.astype(F32)).astype(BF16)
    return high, low


def dot(a, b):
    return jnp.dot(a, b, preferred_element_type=F32)


def left3(pair, value):
    high, low = split(value)
    both = dot(pair, high)
    return both[:B] + both[B:] + dot(pair[:B], low)


def right3(value, t_high, t_low):
    high, low = split(value)
    return dot(high, t_high) + dot(low, t_high) + dot(high, t_low)


def right1(value, table):
    high, low = split(value)
    return dot(high, table) + dot(low, table)


def left1(table, value):
    high, low = split(value)
    return dot(table, high) + dot(table, low)


def iotas(rows, cols):
    return (
        lax.broadcasted_iota(jnp.int32, (rows, cols), 0),
        lax.broadcasted_iota(jnp.int32, (rows, cols), 1),
    )


def band(index):
    one = jnp.int32(1)
    zero = jnp.int32(0)
    total = jnp.zeros_like(index)
    for k in range(1, GROUP):
        total = total + jnp.where(index >= k * B, one, zero)
    return total


def hot(condition):
    return jnp.where(condition, 1.0, 0.0).astype(BF16)


def kernel(
    slabs,
    corners,
    pairs,
    count,
    eigen,
    orb,
    ext,
    left,
    wide_h,
    wide_l,
    narrow_h,
    narrow_l,
    near,
    column,
    level_bc,
    out,
    obx,
    nxt,
    moved,
    spec,
    pencil,
    turned,
    solved,
    win,
    rbk,
    fw,
    exch,
    ret,
    back,
    dz_to,
    dz_from,
    dx_to,
    dx_from,
    put_z,
    get_z,
    put_x,
    get_x,
    load_sem,
    box_s,
    box_r,
    halo_s,
    halo_r,
    one_s,
    one_r,
    one_o,
    two_s,
    two_r,
    two_o,
    ret_s,
    ret_r,
    den_s,
    den_r,
    fld_s,
    fld_r,
):
    slab = lax.axis_index("slab")
    sub = lax.axis_index("sub")
    ahead = lax.rem(slab + 1, slabs)
    behind = lax.rem(slab + slabs - 1, slabs)
    planes = slabs * SX
    orbitals = 2 * slabs

    barrier = pltpu.get_barrier_semaphore()
    load = pltpu.make_async_copy(orb, obx.at[:, :, EDGE : EDGE + ROWS * B], load_sem)
    load.start()
    for who in (ahead, behind):
        pl.semaphore_signal(barrier, inc=1, device_id=(who, sub), device_id_type=MESH)
    for k in range(1, SUBS):
        pl.semaphore_signal(
            barrier, inc=1, device_id=(slab, lax.rem(sub + k, SUBS)), device_id_type=MESH
        )
    pl.semaphore_wait(barrier, 2 + SUBS - 1)

    def box_copy(g):
        return pltpu.make_async_remote_copy(
            src_ref=obx.at[:, :, pl.ds(pl.multiple_of(EDGE + g * LANES, 128), LANES)],
            dst_ref=nxt.at[:, :, pl.ds(pl.multiple_of(g * LANES, 128), LANES)],
            send_sem=box_s.at[g],
            recv_sem=box_r.at[g],
            device_id=(behind, sub),
            device_id_type=MESH,
        )

    def halo_copy(side):
        start = EDGE if side == 0 else ROWS * B
        land = EDGE + ROWS * B if side == 0 else 0
        who = lax.rem(sub + (SUBS - 1 if side == 0 else 1), SUBS)
        return pltpu.make_async_remote_copy(
            src_ref=obx.at[:, :, start : start + EDGE],
            dst_ref=obx.at[:, :, land : land + EDGE],
            send_sem=halo_s.at[side],
            recv_sem=halo_r.at[side],
            device_id=(slab, who),
            device_id_type=MESH,
        )

    def rows_of(g):
        return pl.ds(pl.multiple_of(g * GROUP * ROWS, 8), GROUP * ROWS)

    def one_copy(k, g):
        who = lax.rem(sub + k, SUBS)
        return pltpu.make_async_remote_copy(
            src_ref=spec.at[:, who, rows_of(g)],
            dst_ref=pencil.at[:, sub, rows_of(g)],
            send_sem=one_s.at[k - 1, g],
            recv_sem=one_r.at[k - 1, g],
            device_id=(slab, who),
            device_id_type=MESH,
        )

    def two_copy(k, g):
        who = lax.rem(sub + k, SUBS)
        return pltpu.make_async_remote_copy(
            src_ref=turned.at[:, who, rows_of(g)],
            dst_ref=solved.at[:, sub, rows_of(g)],
            send_sem=two_s.at[k - 1, g],
            recv_sem=two_r.at[k - 1, g],
            device_id=(slab, who),
            device_id_type=MESH,
        )

    def one_own(g):
        return pltpu.make_async_copy(
            spec.at[:, sub, rows_of(g)], pencil.at[:, sub, rows_of(g)], one_o.at[g]
        )

    def two_own(g):
        return pltpu.make_async_copy(
            turned.at[:, sub, rows_of(g)], solved.at[:, sub, rows_of(g)], two_o.at[g]
        )

    def ret_copy(g):
        lanes = pl.ds(pl.multiple_of(g * LANES, 128), LANES)
        return pltpu.make_async_remote_copy(
            src_ref=ret.at[:, :, lanes],
            dst_ref=back.at[:, :, lanes],
            send_sem=ret_s.at[g],
            recv_sem=ret_r.at[g],
            device_id=(ahead, sub),
            device_id_type=MESH,
        )

    def den_copy(step, c):
        lanes = pl.ds(c * RL, RL)
        return pltpu.make_async_remote_copy(
            src_ref=win.at[REACH - step, :, lanes],
            dst_ref=rbk.at[step - 1, :, lanes],
            send_sem=den_s.at[step - 1, c],
            recv_sem=den_r.at[step - 1, c],
            device_id=(ahead, sub),
            device_id_type=MESH,
        )

    def fld_copy(step, c):
        lanes = pl.ds(c * RL, RL)
        return pltpu.make_async_remote_copy(
            src_ref=fw.at[step - 1, :, lanes],
            dst_ref=fw.at[step, :, lanes],
            send_sem=fld_s.at[step - 1, c],
            recv_sem=fld_r.at[step - 1, c],
            device_id=(behind, sub),
            device_id_type=MESH,
        )

    start_x = []
    start_z = []
    for o in range(2):
        mine = slab * 2 + o
        start_x.append(lax.rem(corners[2 * mine] - slab * SX + planes, planes))
        start_z.append(corners[2 * mine + 1])
    first, second, weight, shift_x, shift_z = [], [], [], [], []
    for s in range(2):
        i, j = pairs[s, 0], pairs[s, 1]
        first.append(lax.rem(i - 2 * slab + orbitals, orbitals))
        second.append(lax.rem(j - 2 * slab + orbitals, orbitals))
        half = planes // 2
        shift_x.append(
            lax.rem(corners[2 * j] - corners[2 * i] + half + planes, planes) - half
        )
        shift_z.append(corners[2 * j + 1] - corners[2 * i + 1])
        weight.append(jnp.where(count[0] > s, jnp.float32(1.0), jnp.float32(0.0)))

    load.wait()

    def send_boxes(g, _):
        box_copy(g).start()
        return 0

    lax.fori_loop(0, CHUNKS, send_boxes, 0)
    halo_copy(0).start()
    halo_copy(1).start()

    row, col = iotas(LANES, GLANES)
    at = row + 32 * band(row)
    for o in range(2):
        put_z[o] = hot(col - at == start_z[o])
    row, col = iotas(REACH * SX, B)
    for o in range(2):
        put_x[o] = hot(row - col == start_x[o])

    def deposit(g, _):
        lanes = pl.ds(pl.multiple_of(EDGE + g * LANES, 128), LANES)
        total = None
        for o in range(2):
            box = obx[o, :, lanes]
            wide = right1(box * box, put_z[o])
            part = left1(put_x[o], wide)
            total = part if total is None else total + part
        grid = pl.ds(pl.multiple_of(g * GLANES, 128), GLANES)
        win[:, :, grid] = total.reshape(REACH, SX, GLANES)
        return 0

    lax.fori_loop(0, CHUNKS, deposit, 0)
    for c in range(RING):
        den_copy(1, c).start()

    def density_step(step):
        for c in range(RING):
            lanes = pl.ds(c * RL, RL)
            den_copy(step - 1, c).wait_recv()
            win[REACH - step, :, lanes] += rbk[step - 2, :, lanes]
            den_copy(step, c).start()

    row, col = iotas(LANES, LANES)
    same = band(row) == band(col)
    for s in range(2):
        dz_to[s] = hot(same & (col - row == shift_z[s]))
        dz_from[s] = hot(same & (row - col == shift_z[s]))
    row, col = iotas(B, B)
    for s in range(2):
        dx_to[s] = hot(row - col == shift_x[s])
        dx_from[s] = hot(col - row == shift_x[s])
    row, col = iotas(GLANES, LANES)
    at = col + 32 * band(col)
    for o in range(2):
        get_z[o] = hot(row - at == start_z[o])
    row, col = iotas(B, REACH * SX)
    for o in range(2):
        get_x[o] = hot(col - row == start_x[o])

    def forward(g, _):
        density_step(2 + 2 * g)
        density_step(3 + 2 * g)
        box_copy(g).wait_recv()
        lanes = pl.ds(pl.multiple_of(g * LANES, 128), LANES)
        own = pl.ds(pl.multiple_of(EDGE + g * LANES, 128), LANES)
        for s in range(2):
            boxes = [obx[0, :, own], obx[1, :, own]]
            other = jnp.where(
                second[s] < 2,
                jnp.where(second[s] == 0, boxes[0], boxes[1]),
                jnp.where(second[s] == 2, nxt[0, :, lanes], nxt[1, :, lanes]),
            )
            shifted = left1(dx_to[s], right1(other, dz_to[s]))
            moved[s, :, lanes] = shifted
            rho = jnp.where(first[s] == 0, boxes[0], boxes[1]) * shifted
            wide = right3(rho, wide_h[...], wide_l[...])
            for k in range(0, GROUP, 2):
                two = left3(left[...], wide[:, k * GZ : (k + 2) * GZ])
                for m in range(2):
                    for q in range(SUBS):
                        spec[s, q, pl.ds(pl.multiple_of((g * GROUP + k + m) * ROWS, 8), ROWS), :] = (
                            two[q * ROWS : (q + 1) * ROWS, m * GZ : (m + 1) * GZ]
                        )
        for k in (2, 1, 3):
            one_copy(k, g).start()
        one_own(g).start()
        return 0

    lax.fori_loop(0, CHUNKS, forward, 0)
    density_step(14)
    density_step(15)

    for c in range(RING):
        lanes = pl.ds(c * RL, RL)
        den_copy(15, c).wait_recv()
        value = win[0, :, lanes] + rbk[14, :, lanes] + EPSILON
        root = jnp.exp(jnp.log(value) * (1.0 / 3.0))
        root = root - (root * root * root - value) / (3.0 * root * root)
        fw[0, :, lanes] = ext[:, lanes] - LOCAL_FACTOR * root
        fld_copy(1, c).start()

    def field_step(step):
        for c in range(RING):
            fld_copy(step - 1, c).wait_recv()
            fld_copy(step, c).start()

    def wait_one(g, _):
        for k in range(1, SUBS):
            one_copy(k, g).wait_recv()
        one_own(g).wait()
        return 0

    lax.fori_loop(0, CHUNKS, wait_one, 0)

    def along_y(t, _):
        a = 2 * t
        pieces = []
        for m in range(2):
            level = eigen[sub * ROWS + a + m]
            pieces.append((4.0 * math.pi) / (level_bc[...] + level))
        factor = jnp.concatenate(pieces, axis=1)
        for s in range(2):
            parts = []
            for m in range(2):
                parts.append(
                    jnp.concatenate(
                        [pencil[s, q, pl.ds(a + m, ROWS, stride=ROWS), :] for q in range(SUBS)],
                        axis=0,
                    )
                )
            value = jnp.concatenate(parts, axis=1)
            value = left3(left[...], factor * left3(left[...], value))
            for m in range(2):
                for q in range(SUBS):
                    turned[s, q, pl.ds(a + m, ROWS, stride=ROWS), :] = value[
                        q * ROWS : (q + 1) * ROWS, m * GZ : (m + 1) * GZ
                    ]
        field_step(2 + t)
        return 0

    lax.fori_loop(0, ROWS // 2, along_y, 0)

    def send_two(g, _):
        for k in (2, 1, 3):
            two_copy(k, g).start()
        two_own(g).start()
        return 0

    lax.fori_loop(0, CHUNKS, send_two, 0)
    field_step(14)
    field_step(15)
    halo_copy(0).wait_recv()
    halo_copy(1).wait_recv()
    keep_low = jnp.where(sub > 0, jnp.float32(1.0), jnp.float32(0.0))
    keep_high = jnp.where(sub < SUBS - 1, jnp.float32(1.0), jnp.float32(0.0))
    obx[:, :, 0:EDGE] = obx[:, :, 0:EDGE] * keep_low
    high_edge = EDGE + ROWS * B
    obx[:, :, high_edge : high_edge + EDGE] = obx[:, :, high_edge : high_edge + EDGE] * keep_high

    def inverse(g, _):
        for k in range(1, SUBS):
            two_copy(k, g).wait_recv()
        two_own(g).wait()
        lanes = pl.ds(pl.multiple_of(g * LANES, 128), LANES)
        own = pl.ds(pl.multiple_of(EDGE + g * LANES, 128), LANES)
        boxes = [obx[0, :, own], obx[1, :, own]]
        mine = [None, None]
        theirs = [None, None]

        def add(held, k, value):
            held[k] = value if held[k] is None else held[k] + value

        for s in range(2):
            parts = []
            for k in range(0, GROUP, 2):
                pieces = []
                for m in range(2):
                    rows = pl.ds(pl.multiple_of((g * GROUP + k + m) * ROWS, 8), ROWS)
                    pieces.append(
                        jnp.concatenate([solved[s, q, rows, :] for q in range(SUBS)], axis=0)
                    )
                parts.append(left3(left[...], jnp.concatenate(pieces, axis=1)))
            potential = right3(jnp.concatenate(parts, axis=1), narrow_h[...], narrow_l[...])
            potential = potential * weight[s]
            onto_first = potential * moved[s, :, lanes]
            onto_second = left1(
                dx_from[s], right1(
                    potential * jnp.where(first[s] == 0, boxes[0], boxes[1]), dz_from[s]
                ),

            )
            for k in range(2):
                add(mine, k, jnp.where(first[s] == k, onto_first, 0.0))
                add(mine, k, jnp.where(second[s] == k, onto_second, 0.0))
                add(theirs, k, jnp.where(second[s] == 2 + k, onto_second, 0.0))
        for k in range(2):
            exch[k, :, lanes] = mine[k]
            ret[k, :, lanes] = theirs[k]
        ret_copy(g).start()
        return 0

    lax.fori_loop(0, CHUNKS, inverse, 0)
    for c in range(RING):
        fld_copy(15, c).wait_recv()

    def finish(g, _):
        lanes = pl.ds(pl.multiple_of(g * LANES, 128), LANES)
        own = pl.ds(pl.multiple_of(EDGE + g * LANES, 128), LANES)
        around = pl.ds(pl.multiple_of(g * LANES, 128), LANES + 2 * EDGE)
        grid = pl.ds(pl.multiple_of(g * GLANES, 128), GLANES)
        field = fw[:, :, grid].reshape(REACH * SX, GLANES)
        ret_copy(g).wait_recv()
        for o in range(2):
            box = obx[o, :, own]
            local = right1(left1(get_x[o], field), get_z[o])
            lap = right1(obx[o, :, around], near[...]) + left1(column[...], box)
            out[o, :, lanes] = (
                -0.5 * lap + local * box - FOCK_SHARE * (exch[o, :, lanes] + back[o, :, lanes])
            )
        return 0

    lax.fori_loop(0, CHUNKS, finish, 0)

    def drain(g, _):
        box_copy(g).wait_send()
        ret_copy(g).wait_send()
        for k in range(1, SUBS):
            one_copy(k, g).wait_send()
            two_copy(k, g).wait_send()
        return 0

    lax.fori_loop(0, CHUNKS, drain, 0)
    halo_copy(0).wait_send()
    halo_copy(1).wait_send()

    def drain_ring(step, _):
        for c in range(RING):
            den_copy(step, c).wait_send()
            fld_copy(step, c).wait_send()
        return 0

    lax.fori_loop(1, REACH, drain_ring, 0)


def local(slabs, orbitals, external_potential, corners, pair_list, pair_count):
    vmem = pl.BlockSpec(memory_space=pltpu.VMEM)
    smem = pl.BlockSpec(memory_space=pltpu.SMEM)
    table = tables()
    arrays = [jnp.asarray(t) for t in table[:-1]]
    eigen = jnp.asarray(table[-1])
    dma = pltpu.SemaphoreType.DMA
    part = (2, B, ROWS * B)
    turns = (2, SUBS, ROWS * ROWS, GZ)
    return pl.pallas_call(
        functools.partial(kernel, slabs),
        out_shape=jax.ShapeDtypeStruct(orbitals.shape, F32),
        in_specs=[smem] * 4 + [pl.BlockSpec(memory_space=pl.ANY)] + [vmem] * (1 + len(arrays)),
        out_specs=vmem,
        scratch_shapes=[
            pltpu.VMEM((2, B, ROWS * B + 2 * EDGE), F32),
            pltpu.VMEM(part, F32),
            pltpu.VMEM(part, F32),
            pltpu.VMEM(turns, F32),
            pltpu.VMEM(turns, F32),
            pltpu.VMEM(turns, F32),
            pltpu.VMEM(turns, F32),
            pltpu.VMEM((REACH, SX, ROWS * GZ), F32),
            pltpu.VMEM((REACH - 1, SX, ROWS * GZ), F32),
            pltpu.VMEM((REACH, SX, ROWS * GZ), F32),
            pltpu.VMEM(part, F32),
            pltpu.VMEM(part, F32),
            pltpu.VMEM(part, F32),
            pltpu.VMEM((2, LANES, LANES), BF16),
            pltpu.VMEM((2, LANES, LANES), BF16),
            pltpu.VMEM((2, B, B), BF16),
            pltpu.VMEM((2, B, B), BF16),
            pltpu.VMEM((2, LANES, GLANES), BF16),
            pltpu.VMEM((2, GLANES, LANES), BF16),
            pltpu.VMEM((2, REACH * SX, B), BF16),
            pltpu.VMEM((2, B, REACH * SX), BF16),
            dma,
            dma((CHUNKS,)),
            dma((CHUNKS,)),
            dma((2,)),
            dma((2,)),
            dma((SUBS - 1, CHUNKS)),
            dma((SUBS - 1, CHUNKS)),
            dma((CHUNKS,)),
            dma((SUBS - 1, CHUNKS)),
            dma((SUBS - 1, CHUNKS)),
            dma((CHUNKS,)),
            dma((CHUNKS,)),
            dma((CHUNKS,)),
            dma((REACH - 1, RING)),
            dma((REACH - 1, RING)),
            dma((REACH - 1, RING)),
            dma((REACH - 1, RING)),
        ],
        compiler_params=pltpu.CompilerParams(
            collective_id=0, has_side_effects=True, vmem_limit_bytes=60 * 1024 * 1024
        ),
        name="orbitals",
    )(corners.reshape(-1), pair_list, pair_count, eigen, orbitals, external_potential, *arrays)


def solution(mesh):
    placed = (P("slab", None, "sub"), P("slab", "sub"), P(), P("slab", None), P("slab"))
    return jax.shard_map(
        functools.partial(local, mesh.shape["slab"]),
        mesh=mesh,
        in_specs=placed,
        out_specs=P("slab", None, "sub"),
        check_vma=False,
    )
```

profile of v0, /device:TPU:6, one launch (start us, length us, event | category | flops | bytes accessed | tf_op | source)
XLA Modules:
  0.0 120.8 jit_solution(481680516352300970)
XLA Ops:
  0.7 0.8 copy.15
  1.5 0.7 reshape.3.corners
  2.2 115.8 %orbitals.1 = f32[2,96,2304]{2,1,0:T(8,128)} custom-call(s32[512]{0:T(512)} %reshape.3.corners, s32[2,2]{1,0:T(2,128)} %pairs.1, s32[1]{0:T(128)S(6)} %copy.17.count, f32[96]{0:T(128)} %constant.26.clone.eigen, f32[2,96,2304]{2,1,0:T(8,128)} %orb.1, f32[8,3072]{1,0:T(8,128)} %ext.1, bf16[192,96]{1,0:T(8,128)(2,1)} %constant.18.clone.left, ...), custom_call_target="tpu_custom_call" | custom-call | tf_op jit(solution)/shard_map/orbitals/pallas_call | solution.py:562
  118.0 2.8 %copy.18 = f32[2,96,2304]{2,1,0:T(8,128)} copy(f32[2,96,2304]{2,1,0:T(8,128)} %orbitals.1) | data formatting | bytes 3538944
where the time goes:
time: 121 us
  Pallas kernels  116 us (96%)
  local copies, waits for them, and re-layouts  4.33 us (4%)
    pallas_call x1, Pallas kernels, local(): pl.pallas_call(functools.partial(kernel, slabs), out_shape=jax.ShapeDtype...  116 us
    unnamed x2, local copies, waits for them, and re-layouts  3.61 us

commit v1 on v0

v1 whole, which is shorter than its diff:
```python
import functools
import math

import jax
import jax.numpy as jnp
import ml_dtypes
import numpy as np
from jax import lax
from jax.experimental import pallas as pl
from jax.experimental.pallas import tpu as pltpu
from jax.sharding import PartitionSpec as P

SCREEN = 0.0008
FOCK_SHARE = 0.25
LOCAL_FACTOR = (3.0 / math.pi) ** (1.0 / 3.0)
EPSILON = 1e-06

B = 96
ROWS = 24
GZ = 128
SX = 8
REACH = 16
SUBS = 4
GROUP = 4
CHUNKS = ROWS // GROUP
LANES = GROUP * B
GLANES = GROUP * GZ
EDGE = 128
RING = 3
RL = ROWS * GZ // RING
HOPS = REACH // 2
OCTS = ROWS // 8

F32 = jnp.float32
BF16 = jnp.bfloat16
MESH = pl.DeviceIdType.MESH


def halves(value):
    high = value.astype(ml_dtypes.bfloat16)
    low = (value - high.astype(np.float64)).astype(ml_dtypes.bfloat16)
    return high, low


def tables():
    level = np.arange(B, dtype=np.float64) + 1.0
    sine = math.sqrt(2.0 / (B + 1)) * np.sin(math.pi * level[:, None] * level[None, :] / (B + 1))
    eigen = 2.0 - 2.0 * np.cos(math.pi * level / (B + 1))
    high, low = halves(sine)
    left = np.block([[high, high], [low, np.zeros_like(low)]])
    wide = np.zeros((LANES, GLANES), np.float64)
    for k in range(GROUP):
        wide[k * B : (k + 1) * B, k * GZ : k * GZ + B] = sine
    wide_high, wide_low = halves(wide)
    narrow_high, narrow_low = wide_high.T.copy(), wide_low.T.copy()
    rows = np.arange(LANES + 2 * EDGE)[:, None] - EDGE
    cols = np.arange(LANES)[None, :]
    beside = np.abs(rows - cols)
    near = (beside == B) | ((beside == 1) & (rows // B == cols // B))
    near = near.astype(ml_dtypes.bfloat16)
    line = np.abs(np.arange(B)[:, None] - np.arange(B)[None, :])
    column = ((line == 1) * 1.0 - (line == 0) * 6.0).astype(ml_dtypes.bfloat16)
    column = np.concatenate([column, column], axis=1)
    level_bc = np.ones((B, GZ), np.float64)
    level_bc[:, :B] = eigen[:, None] + eigen[None, :] + SCREEN
    return (
        left,
        wide_high,
        wide_low,
        narrow_high,
        narrow_low,
        near,
        column,
        level_bc.astype(np.float32),
        eigen.astype(np.float32),
    )


def split(value):
    high = value.astype(BF16)
    low = (value - high.astype(F32)).astype(BF16)
    return high, low


def stack(value):
    return jnp.concatenate(split(value), axis=0)


def dot(a, b):
    return jnp.dot(a, b, preferred_element_type=F32)


def left3(table, value):
    both = dot(table, stack(value))
    return both[:B] + both[B:]


def right3(values, t_high, t_low):
    parts = [split(v) for v in values]
    rows = values[0].shape[0]
    count = len(values)
    high = jnp.concatenate([p[0] for p in parts], axis=0)
    full = dot(jnp.concatenate([high] + [p[1] for p in parts], axis=0), t_high)
    rest = dot(high, t_low)
    return [
        full[k * rows : (k + 1) * rows]
        + full[(count + k) * rows : (count + k + 1) * rows]
        + rest[k * rows : (k + 1) * rows]
        for k in range(count)
    ]


def right1(value, table):
    rows = value.shape[0]
    both = dot(stack(value), table)
    return both[:rows] + both[rows:]


def pick1(value, table):
    return dot(stack(value), table).astype(BF16)


def iotas(rows, cols):
    return (
        lax.broadcasted_iota(jnp.int32, (rows, cols), 0),
        lax.broadcasted_iota(jnp.int32, (rows, cols), 1),
    )


def band(index):
    one = jnp.int32(1)
    zero = jnp.int32(0)
    total = jnp.zeros_like(index)
    for k in range(1, GROUP):
        total = total + jnp.where(index >= k * B, one, zero)
    return total


def hot(condition):
    return jnp.where(condition, 1.0, 0.0).astype(BF16)


def twice(table):
    return jnp.concatenate([table, table], axis=1)


def kernel(
    slabs,
    corners,
    pairs,
    count,
    eigen,
    orb,
    ext,
    left,
    wide_h,
    wide_l,
    narrow_h,
    narrow_l,
    near,
    column,
    level_bc,
    out,
    obx,
    nxt,
    moved,
    spec,
    pencil,
    turned,
    solved,
    win,
    mate,
    came,
    fw,
    ret,
    back,
    dz_to,
    dz_from,
    dx_to,
    dx_from,
    put_z,
    get_z,
    put_x,
    get_x,
    load_sem,
    box_s,
    box_r,
    halo_s,
    halo_r,
    one_s,
    one_r,
    one_o,
    two_s,
    two_r,
    two_o,
    ret_s,
    ret_r,
    mate_s,
    mate_r,
    den_s,
    den_r,
    fld_s,
    fld_r,
    give_s,
    give_r,
):
    slab = lax.axis_index("slab")
    sub = lax.axis_index("sub")
    ahead = lax.rem(slab + 1, slabs)
    behind = lax.rem(slab + slabs - 1, slabs)
    ahead2 = lax.rem(slab + 2, slabs)
    behind2 = lax.rem(slab + slabs - 2, slabs)
    odd = lax.rem(slab, 2)
    partner = slab + 1 - 2 * odd
    planes = slabs * SX
    orbitals = 2 * slabs

    load = pltpu.make_async_copy(orb, obx.at[:, :, EDGE : EDGE + ROWS * B], load_sem)
    load.start()
    mate[0] = jnp.zeros((SX, ROWS * GZ), F32)
    mate[HOPS] = jnp.zeros((SX, ROWS * GZ), F32)
    win[REACH] = jnp.zeros((SX, ROWS * GZ), F32)
    barrier = pltpu.get_barrier_semaphore()
    for who in (ahead, behind, ahead2, behind2):
        pl.semaphore_signal(barrier, inc=1, device_id=(who, sub), device_id_type=MESH)
    for k in range(1, SUBS):
        pl.semaphore_signal(
            barrier, inc=1, device_id=(slab, lax.rem(sub + k, SUBS)), device_id_type=MESH
        )

    def remote(src, dst, send, recv, who):
        return pltpu.make_async_remote_copy(
            src_ref=src,
            dst_ref=dst,
            send_sem=send,
            recv_sem=recv,
            device_id=who,
            device_id_type=MESH,
        )

    def box_lanes(g):
        return pl.ds(pl.multiple_of(g * LANES, 128), LANES)

    def own_lanes(g):
        return pl.ds(pl.multiple_of(EDGE + g * LANES, 128), LANES)

    def grid_lanes(g):
        return pl.ds(pl.multiple_of(g * GLANES, 128), GLANES)

    def box_copy(g):
        return remote(
            obx.at[:, :, own_lanes(g)],
            nxt.at[:, :, box_lanes(g)],
            box_s,
            box_r.at[g],
            (behind, sub),
        )

    def halo_copy(side):
        start = EDGE if side == 0 else ROWS * B
        land = EDGE + ROWS * B if side == 0 else 0
        who = lax.rem(sub + (SUBS - 1 if side == 0 else 1), SUBS)
        return remote(
            obx.at[:, :, start : start + EDGE],
            obx.at[:, :, land : land + EDGE],
            halo_s.at[side],
            halo_r.at[side],
            (slab, who),
        )

    def rows_of(g):
        return pl.ds(pl.multiple_of(g * GROUP * ROWS, 8), GROUP * ROWS)

    def one_copy(k, g):
        who = lax.rem(sub + k, SUBS)
        return remote(
            spec.at[:, who, rows_of(g)],
            pencil.at[:, sub, rows_of(g)],
            one_s.at[k - 1],
            one_r.at[k - 1, g],
            (slab, who),
        )

    def one_own(g):
        return pltpu.make_async_copy(
            spec.at[:, sub, rows_of(g)], pencil.at[:, sub, rows_of(g)], one_o.at[g]
        )

    def piece(e, g):
        if g is None:
            return pl.ds(0, ROWS * 8)
        return pl.ds(pl.multiple_of(g * GROUP * 8, 8), GROUP * 8)

    def slot(e, g):
        return e if g is None else OCTS - 1 + g

    def two_copy(k, e, g):
        who = lax.rem(sub + k, SUBS)
        return remote(
            turned.at[:, who, e, piece(e, g)],
            solved.at[:, sub, e, piece(e, g)],
            two_s.at[k - 1],
            two_r.at[k - 1, slot(e, g)],
            (slab, who),
        )

    def two_own(e, g):
        return pltpu.make_async_copy(
            turned.at[:, sub, e, piece(e, g)],
            solved.at[:, sub, e, piece(e, g)],
            two_o.at[slot(e, g)],
        )

    def two_send(e, g):
        for k in (2, 1, 3):
            two_copy(k, e, g).start()
        two_own(e, g).start()

    def two_wait(e, g):
        for k in range(1, SUBS):
            two_copy(k, e, g).wait_recv()
        two_own(e, g).wait()

    def ret_copy(g):
        return remote(
            ret.at[:, :, box_lanes(g)],
            back.at[:, :, box_lanes(g)],
            ret_s,
            ret_r.at[g],
            (ahead, sub),
        )

    def mate_copy(k):
        return remote(
            win.at[2 * k + 1],
            mate.at[k + odd],
            mate_s,
            mate_r.at[k],
            (partner, sub),
        )

    def ring(c):
        return pl.ds(c * RL, RL)

    def den_copy(j, c):
        return remote(
            win.at[2 * (HOPS + 1 - j), :, ring(c)],
            came.at[HOPS - j, :, ring(c)],
            den_s,
            den_r.at[j - 1, c],
            (ahead2, sub),
        )

    def fld_copy(j, c):
        return remote(
            fw.at[2 * j - 1, :, ring(c)],
            fw.at[2 * j + 1, :, ring(c)],
            fld_s,
            fld_r.at[j - 1, c],
            (behind2, sub),
        )

    def give_copy(j):
        return remote(
            fw.at[2 * j + 1],
            fw.at[2 * j + 2 * odd],
            give_s,
            give_r.at[j],
            (partner, sub),
        )

    start_x = []
    start_z = []
    for o in range(2):
        mine = slab * 2 + o
        start_x.append(lax.rem(corners[0, mine] - slab * SX + planes, planes))
        start_z.append(corners[1, mine])
    first, second, weight, shift_x, shift_z = [], [], [], [], []
    for s in range(2):
        i, j = pairs[s, 0], pairs[s, 1]
        first.append(lax.rem(i - 2 * slab + orbitals, orbitals))
        second.append(lax.rem(j - 2 * slab + orbitals, orbitals))
        half = planes // 2
        shift_x.append(lax.rem(corners[0, j] - corners[0, i] + half + planes, planes) - half)
        shift_z.append(corners[1, j] - corners[1, i])
        weight.append(jnp.where(count[0] > s, jnp.float32(1.0), jnp.float32(0.0)))

    row, col = iotas(LANES, GLANES)
    at = col - row - 32 * band(row)
    for o in range(2):
        put_z[o] = hot(at == start_z[o])
    row, col = iotas(REACH * SX, B)
    at = row - col
    for o in range(2):
        put_x[:, 2 * o * B : (2 * o + 2) * B] = twice(hot(at == start_x[o]))

    pl.semaphore_wait(barrier, 4 + SUBS - 1)
    load.wait()

    def send_boxes(g, _):
        box_copy(g).start()
        return 0

    lax.fori_loop(0, CHUNKS, send_boxes, 0)
    halo_copy(0).start()
    halo_copy(1).start()

    def deposit(g, _):
        parts = []
        for o in range(2):
            box = obx[o, :, own_lanes(g)]
            parts.append(pick1(box * box, put_z[o]))
        total = dot(put_x[...], jnp.concatenate(parts, axis=0))
        win[0:REACH, :, grid_lanes(g)] = total.reshape(REACH, SX, GLANES)
        return 0

    lax.fori_loop(0, CHUNKS, deposit, 0)

    def send_mate(k, _):
        mate_copy(HOPS - 1 - k).start()
        return 0

    lax.fori_loop(0, HOPS, send_mate, 0)

    row, col = iotas(LANES, LANES)
    same = band(row) == band(col)
    at = col - row
    for s in range(2):
        dz_to[s] = hot(same & (at == shift_z[s]))
        dz_from[s] = hot(same & (at == -shift_z[s]))
    row, col = iotas(B, B)
    at = row - col
    for s in range(2):
        dx_to[s] = twice(hot(at == shift_x[s]))
        dx_from[s] = twice(hot(at == -shift_x[s]))
    row, col = iotas(GLANES, LANES)
    at = row - col - 32 * band(col)
    for o in range(2):
        get_z[o] = hot(at == start_z[o])
    row, col = iotas(B, REACH * SX)
    at = col - row
    for o in range(2):
        get_x[o * B : (o + 1) * B, :] = twice(hot(at == start_x[o]))

    mate_copy(HOPS - 1).wait_recv()
    for c in range(RING):
        win[REACH, :, ring(c)] += mate[HOPS, :, ring(c)]
        den_copy(1, c).start()

    def density_step(j):
        m = HOPS + 1 - j
        mate_copy(HOPS - j).wait_recv()
        for c in range(RING):
            den_copy(j - 1, c).wait_recv()
            win[2 * m, :, ring(c)] += mate[m, :, ring(c)] + came[m, :, ring(c)]
            den_copy(j, c).start()

    halo_copy(0).wait_recv()
    halo_copy(1).wait_recv()
    keep_low = jnp.where(sub > 0, jnp.float32(1.0), jnp.float32(0.0))
    keep_high = jnp.where(sub < SUBS - 1, jnp.float32(1.0), jnp.float32(0.0))
    obx[:, :, 0:EDGE] = obx[:, :, 0:EDGE] * keep_low
    high_edge = EDGE + ROWS * B
    obx[:, :, high_edge : high_edge + EDGE] = obx[:, :, high_edge : high_edge + EDGE] * keep_high

    def forward(g, _):
        density_step(2 + g)
        parts = [split(obx[o, :, pl.ds(pl.multiple_of(g * LANES, 128), LANES + 2 * EDGE)]) for o in range(2)]
        beside = dot(
            jnp.concatenate([p[0] for p in parts] + [p[1] for p in parts], axis=0), near[...]
        )
        for o in range(2):
            inner = [p[:, EDGE : EDGE + LANES] for p in parts[o]]
            lap = dot(column[...], jnp.concatenate(inner, axis=0))
            lap = lap + beside[o * B : (o + 1) * B] + beside[(2 + o) * B : (3 + o) * B]
            out[o, :, box_lanes(g)] = -0.5 * lap
        box_copy(g).wait_recv()
        boxes = [obx[0, :, own_lanes(g)], obx[1, :, own_lanes(g)]]
        later = [nxt[0, :, box_lanes(g)], nxt[1, :, box_lanes(g)]]
        rhos = []
        for s in range(2):
            other = jnp.where(
                second[s] < 2,
                jnp.where(second[s] == 0, boxes[0], boxes[1]),
                jnp.where(second[s] == 2, later[0], later[1]),
            )
            shifted = dot(dx_to[s], pick1(other, dz_to[s]))
            moved[s, :, box_lanes(g)] = shifted
            rhos.append(jnp.where(first[s] == 0, boxes[0], boxes[1]) * shifted)
        wides = right3(rhos, wide_h[...], wide_l[...])
        for s in range(2):
            for k in range(0, GROUP, 2):
                two = left3(left[...], wides[s][:, k * GZ : (k + 2) * GZ])
                for m in range(2):
                    rows = pl.ds(pl.multiple_of((g * GROUP + k + m) * ROWS, 8), ROWS)
                    for q in range(SUBS):
                        spec[s, q, rows, :] = two[
                            q * ROWS : (q + 1) * ROWS, m * GZ : (m + 1) * GZ
                        ]
        for k in (2, 1, 3):
            one_copy(k, g).start()
        one_own(g).start()
        return 0

    lax.fori_loop(0, CHUNKS, forward, 0)
    density_step(HOPS)

    for c in range(RING):
        den_copy(HOPS, c).wait_recv()
        value = win[0, :, ring(c)] + mate[0, :, ring(c)] + came[0, :, ring(c)] + EPSILON
        root = jnp.exp(jnp.log(value) * (1.0 / 3.0))
        root = root - (root * root * root - value) / (3.0 * root * root)
        fw[1, :, ring(c)] = ext[:, ring(c)] - LOCAL_FACTOR * root
        fld_copy(1, c).start()
    give_copy(0).start()

    def field_last():
        for c in range(RING):
            fld_copy(HOPS, c).wait_recv()
        give_copy(HOPS).start()

    def field_step(j):
        for c in range(RING):
            fld_copy(j, c).wait_recv()
            fld_copy(j + 1, c).start()
        give_copy(j).start()

    def wait_one(g, _):
        for k in range(1, SUBS):
            one_copy(k, g).wait_recv()
        one_own(g).wait()
        return 0

    lax.fori_loop(0, CHUNKS, wait_one, 0)

    def along_y(e, t):
        a = 2 * t
        pieces = []
        for m in range(2):
            level = eigen[sub * ROWS + 8 * e + a + m]
            pieces.append((4.0 * math.pi) / (level_bc[...] + level))
        factor = jnp.concatenate(pieces, axis=1)
        for s in range(2):
            parts = []
            for m in range(2):
                parts.append(
                    jnp.concatenate(
                        [
                            pencil[s, q, pl.ds(8 * e + a + m, ROWS, stride=ROWS), :]
                            for q in range(SUBS)
                        ],
                        axis=0,
                    )
                )
            value = jnp.concatenate(parts, axis=1)
            value = left3(left[...], factor * left3(left[...], value))
            for m in range(2):
                for q in range(SUBS):
                    turned[s, q, e, pl.ds(a + m, ROWS, stride=8), :] = value[
                        q * ROWS : (q + 1) * ROWS, m * GZ : (m + 1) * GZ
                    ]

    def octet(e, _):
        def turn(t, _):
            along_y(e, t)
            return 0

        lax.fori_loop(0, 4, turn, 0)
        two_send(e, None)
        field_step(1 + e)
        return 0

    lax.fori_loop(0, OCTS - 1, octet, 0)

    def turn_last(t, _):
        along_y(OCTS - 1, t)
        return 0

    lax.fori_loop(0, 4, turn_last, 0)

    def send_two(g, _):
        two_send(OCTS - 1, g)
        return 0

    lax.fori_loop(0, CHUNKS, send_two, 0)
    for e in range(OCTS - 1):
        two_wait(e, None)

    def inverse(g, _):
        two_wait(OCTS - 1, g)
        boxes = [obx[0, :, own_lanes(g)], obx[1, :, own_lanes(g)]]
        mine = [None, None]
        theirs = [None, None]

        def add(held, k, value):
            held[k] = value if held[k] is None else held[k] + value

        wides = []
        for s in range(2):
            parts = []
            for k in range(0, GROUP, 2):
                pieces = []
                for m in range(2):
                    rows = pl.ds(pl.multiple_of((g * GROUP + k + m) * 8, 8), 8)
                    pieces.append(
                        jnp.concatenate(
                            [solved[s, q, e, rows, :] for q in range(SUBS) for e in range(OCTS)],
                            axis=0,
                        )
                    )
                parts.append(left3(left[...], jnp.concatenate(pieces, axis=1)))
            wides.append(jnp.concatenate(parts, axis=1))
        potentials = right3(wides, narrow_h[...], narrow_l[...])
        for s in range(2):
            potential = potentials[s] * (weight[s] * FOCK_SHARE)
            onto_first = potential * moved[s, :, box_lanes(g)]
            onto_second = dot(
                dx_from[s],
                pick1(potential * jnp.where(first[s] == 0, boxes[0], boxes[1]), dz_from[s]),
            )
            for k in range(2):
                add(mine, k, jnp.where(first[s] == k, onto_first, 0.0))
                add(mine, k, jnp.where(second[s] == k, onto_second, 0.0))
                add(theirs, k, jnp.where(second[s] == 2 + k, onto_second, 0.0))
        for k in range(2):
            out[k, :, box_lanes(g)] -= mine[k]
            ret[k, :, box_lanes(g)] = theirs[k]
        ret_copy(g).start()
        return 0

    def inverse_step(g, _):
        field_step(OCTS + g)
        return inverse(g, _)

    lax.fori_loop(0, CHUNKS - 1, inverse_step, 0)
    field_last()
    inverse(CHUNKS - 1, 0)

    def wait_give(j, _):
        give_copy(j).wait_recv()
        return 0

    lax.fori_loop(0, HOPS + 1, wait_give, 0)

    def finish(g, _):
        field = fw[1 : REACH + 1, :, grid_lanes(g)].reshape(REACH * SX, GLANES)
        local = dot(get_x[...], stack(field))
        ret_copy(g).wait_recv()
        for o in range(2):
            here = right1(local[o * B : (o + 1) * B], get_z[o])
            out[o, :, box_lanes(g)] += (
                here * obx[o, :, own_lanes(g)] - back[o, :, box_lanes(g)]
            )
        return 0

    lax.fori_loop(0, CHUNKS, finish, 0)

    remote(obx.at[:, :, EDGE : EDGE + ROWS * B], nxt, box_s, box_r.at[0], (behind, sub)).wait_send()
    remote(ret, back, ret_s, ret_r.at[0], (ahead, sub)).wait_send()
    for k in range(1, SUBS):
        who = lax.rem(sub + k, SUBS)
        remote(spec.at[:, who], pencil.at[:, sub], one_s.at[k - 1], one_r.at[0, 0], (slab, who)).wait_send()
        remote(turned.at[:, who], solved.at[:, sub], two_s.at[k - 1], two_r.at[0, 0], (slab, who)).wait_send()
    halo_copy(0).wait_send()
    halo_copy(1).wait_send()
    eight = win.at[0:HOPS]
    nine = win.at[0 : HOPS + 1]
    remote(eight, came, mate_s, mate_r.at[0], (partner, sub)).wait_send()
    remote(eight, came, den_s, den_r.at[0, 0], (ahead2, sub)).wait_send()
    remote(eight, came, fld_s, fld_r.at[0, 0], (behind2, sub)).wait_send()
    remote(nine, mate, give_s, give_r.at[0], (partner, sub)).wait_send()


def local(slabs, orbitals, external_potential, corners, pair_list, pair_count):
    vmem = pl.BlockSpec(memory_space=pltpu.VMEM)
    smem = pl.BlockSpec(memory_space=pltpu.SMEM)
    table = tables()
    arrays = [jnp.asarray(t) for t in table[:-1]]
    eigen = jnp.asarray(table[-1])
    dma = pltpu.SemaphoreType.DMA
    part = (2, B, ROWS * B)
    turns = (2, SUBS, ROWS * ROWS, GZ)
    octs = (2, SUBS, OCTS, ROWS * 8, GZ)
    block = (SX, ROWS * GZ)
    return pl.pallas_call(
        functools.partial(kernel, slabs),
        out_shape=jax.ShapeDtypeStruct(orbitals.shape, F32),
        in_specs=[smem] * 4 + [pl.BlockSpec(memory_space=pl.ANY)] + [vmem] * (1 + len(arrays)),
        out_specs=vmem,
        scratch_shapes=[
            pltpu.VMEM((2, B, ROWS * B + 2 * EDGE), F32),
            pltpu.VMEM(part, F32),
            pltpu.VMEM(part, F32),
            pltpu.VMEM(turns, F32),
            pltpu.VMEM(turns, F32),
            pltpu.VMEM(octs, F32),
            pltpu.VMEM(octs, F32),
            pltpu.VMEM((REACH + 1,) + block, F32),
            pltpu.VMEM((HOPS + 1,) + block, F32),
            pltpu.VMEM((HOPS,) + block, F32),
            pltpu.VMEM((REACH + 3,) + block, F32),
            pltpu.VMEM(part, F32),
            pltpu.VMEM(part, F32),
            pltpu.VMEM((2, LANES, LANES), BF16),
            pltpu.VMEM((2, LANES, LANES), BF16),
            pltpu.VMEM((2, B, 2 * B), BF16),
            pltpu.VMEM((2, B, 2 * B), BF16),
            pltpu.VMEM((2, LANES, GLANES), BF16),
            pltpu.VMEM((2, GLANES, LANES), BF16),
            pltpu.VMEM((REACH * SX, 4 * B), BF16),
            pltpu.VMEM((2 * B, 2 * REACH * SX), BF16),
            dma,
            dma,
            dma((CHUNKS,)),
            dma((2,)),
            dma((2,)),
            dma((SUBS - 1,)),
            dma((SUBS - 1, CHUNKS)),
            dma((CHUNKS,)),
            dma((SUBS - 1,)),
            dma((SUBS - 1, OCTS - 1 + CHUNKS)),
            dma((OCTS - 1 + CHUNKS,)),
            dma,
            dma((CHUNKS,)),
            dma,
            dma((HOPS,)),
            dma,
            dma((HOPS, RING)),
            dma,
            dma((HOPS, RING)),
            dma,
            dma((HOPS + 1,)),
        ],
        compiler_params=pltpu.CompilerParams(
            collective_id=0, has_side_effects=True, vmem_limit_bytes=60 * 1024 * 1024
        ),
        name="orbitals",
    )(corners.T, pair_list, pair_count, eigen, orbitals, external_potential, *arrays)


def solution(mesh):
    placed = (P("slab", None, "sub"), P("slab", "sub"), P(), P("slab", None), P("slab"))
    return jax.shard_map(
        functools.partial(local, mesh.shape["slab"]),
        mesh=mesh,
        in_specs=placed,
        out_specs=P("slab", None, "sub"),
        check_vma=False,
    )
```

time: 121 us -> 106 us (0.88)
  Pallas kernels: 116 us -> 102 us
  local copies, waits for them, and re-layouts: 4.33 us -> 2.8 us
    pallas_call x1, Pallas kernels: 116 us -> 102 us  [local(): pl.pallas_call(functools.partial(kernel, slabs), out_shape=jax.ShapeDtype...]
    unnamed x2 -> x1, local copies, waits for them, and re-layouts: 3.61 us -> 2.8 us
where the time goes in v1:
time: 106 us
  Pallas kernels  102 us (96%)
  local copies, waits for them, and re-layouts  2.8 us (3%)
    pallas_call x1, Pallas kernels, local(): pl.pallas_call(functools.partial(kernel, slabs), out_shape=jax.ShapeDtype...  102 us
    unnamed x1, local copies, waits for them, and re-layouts  2.8 us

profile of v1, /device:TPU:6, one launch (start us, length us, event | category | flops | bytes accessed | tf_op | source)
XLA Modules:
  0.0 105.7 jit_solution(8225293800673769068)
XLA Ops:
  0.7 102.3 %orbitals.1 = f32[2,96,2304]{2,1,0:T(8,128)} custom-call(s32[2,256]{1,0:T(2,128)} %bitcast.1, s32[2,2]{1,0:T(2,128)} %pairs.1, s32[1]{0:T(128)S(6)} %copy.16.count, f32[96]{0:T(128)} %constant.26.clone.eigen, f32[2,96,2304]{2,1,0:T(8,128)} %orb.1, f32[8,3072]{1,0:T(8,128)} %ext.1, bf16[192,192]{1,0:T(8,128)(2,1)} %constant.18.clone.left, ...), custom_call_target="tpu_custom_call" | custom-call | tf_op jit(solution)/shard_map/orbitals/pallas_call | solution.py:685
  102.9 2.8 %copy.17 = f32[2,96,2304]{2,1,0:T(8,128)} copy(f32[2,96,2304]{2,1,0:T(8,128)} %orbitals.1) | data formatting | bytes 3538944

commit v2 on v1

--- a/solution.py
+++ b/solution.py
@@ -29,7 +29,8 @@
 RING = 3
 RL = ROWS * GZ // RING
 HOPS = REACH // 2
-OCTS = ROWS // 8
+PACK = LANES // 128
+SLICE = PACK * ROWS
 
 F32 = jnp.float32
 BF16 = jnp.bfloat16
@@ -48,9 +49,15 @@
     eigen = 2.0 - 2.0 * np.cos(math.pi * level / (B + 1))
     high, low = halves(sine)
     left = np.block([[high, high], [low, np.zeros_like(low)]])
-    wide = np.zeros((LANES, GLANES), np.float64)
+    wide = np.zeros((LANES, LANES), np.float64)
     for k in range(GROUP):
-        wide[k * B : (k + 1) * B, k * GZ : k * GZ + B] = sine
+        lane = np.arange(B)
+        place = k * 128 + lane if k < PACK else (lane // 32) * 128 + B + lane % 32
+        wide[k * B : (k + 1) * B, place] = sine
+    order = np.array([q * ROWS + GROUP * g + k for k in range(GROUP) for q in range(SUBS) for g in range(CHUNKS)])
+    zero = np.zeros_like(low)
+    into = np.block([[high[:, order], high[:, order]], [low[:, order], zero]])
+    outof = np.block([[high[order], high[order]], [low[order], zero]])
     wide_high, wide_low = halves(wide)
     narrow_high, narrow_low = wide_high.T.copy(), wide_low.T.copy()
     rows = np.arange(LANES + 2 * EDGE)[:, None] - EDGE
@@ -65,6 +72,8 @@
     level_bc[:, :B] = eigen[:, None] + eigen[None, :] + SCREEN
     return (
         left,
+        into,
+        outof,
         wide_high,
         wide_low,
         narrow_high,
@@ -153,6 +162,8 @@
     orb,
     ext,
     left,
+    into,
+    outof,
     wide_h,
     wide_l,
     narrow_h,
@@ -174,6 +185,8 @@
     fw,
     ret,
     back,
+    flag,
+    told,
     dz_to,
     dz_from,
     dx_to,
@@ -195,6 +208,8 @@
     two_o,
     ret_s,
     ret_r,
+    flag_s,
+    flag_r,
     mate_s,
     mate_r,
     den_s,
@@ -249,7 +264,7 @@
 
     def box_copy(g):
         return remote(
-            obx.at[:, :, own_lanes(g)],
+            orb.at[:, :, box_lanes(g)],
             nxt.at[:, :, box_lanes(g)],
             box_s,
             box_r.at[g],
@@ -268,67 +283,56 @@
             (slab, who),
         )
 
-    def rows_of(g):
-        return pl.ds(pl.multiple_of(g * GROUP * ROWS, 8), GROUP * ROWS)
-
-    def one_copy(k, g):
+    def spec_rows(g):
+        return pl.ds(pl.multiple_of(g * SLICE, 8), SLICE)
+
+    def pencil_rows(g):
+        return pl.ds(pl.multiple_of((sub * CHUNKS + g) * SLICE, 8), SLICE)
+
+    def one_copy(k, s, g):
         who = lax.rem(sub + k, SUBS)
         return remote(
-            spec.at[:, who, rows_of(g)],
-            pencil.at[:, sub, rows_of(g)],
+            spec.at[s, who, spec_rows(g)],
+            pencil.at[s, pencil_rows(g)],
             one_s.at[k - 1],
-            one_r.at[k - 1, g],
+            one_r.at[k - 1, s, g],
             (slab, who),
         )
 
-    def one_own(g):
+    def one_own(s, g):
         return pltpu.make_async_copy(
-            spec.at[:, sub, rows_of(g)], pencil.at[:, sub, rows_of(g)], one_o.at[g]
-        )
-
-    def piece(e, g):
-        if g is None:
-            return pl.ds(0, ROWS * 8)
-        return pl.ds(pl.multiple_of(g * GROUP * 8, 8), GROUP * 8)
-
-    def slot(e, g):
-        return e if g is None else OCTS - 1 + g
-
-    def two_copy(k, e, g):
+            spec.at[s, sub, spec_rows(g)], pencil.at[s, pencil_rows(g)], one_o.at[s, g]
+        )
+
+    def turned_rows(who, g):
+        return pl.ds(pl.multiple_of((who * CHUNKS + g) * SLICE, 8), SLICE)
+
+    def two_copy(k, s, g):
         who = lax.rem(sub + k, SUBS)
         return remote(
-            turned.at[:, who, e, piece(e, g)],
-            solved.at[:, sub, e, piece(e, g)],
+            turned.at[s, turned_rows(who, g)],
+            solved.at[s, sub, spec_rows(g)],
             two_s.at[k - 1],
-            two_r.at[k - 1, slot(e, g)],
+            two_r.at[k - 1, s, g],
             (slab, who),
         )
 
-    def two_own(e, g):
+    def two_own(s, g):
         return pltpu.make_async_copy(
-            turned.at[:, sub, e, piece(e, g)],
-            solved.at[:, sub, e, piece(e, g)],
-            two_o.at[slot(e, g)],
-        )
-
-    def two_send(e, g):
-        for k in (2, 1, 3):
-            two_copy(k, e, g).start()
-        two_own(e, g).start()
-
-    def two_wait(e, g):
-        for k in range(1, SUBS):
-            two_copy(k, e, g).wait_recv()
-        two_own(e, g).wait()
-
-    def ret_copy(g):
-        return remote(
-            ret.at[:, :, box_lanes(g)],
-            back.at[:, :, box_lanes(g)],
+            turned.at[s, turned_rows(sub, g)], solved.at[s, sub, spec_rows(g)], two_o.at[s, g]
+        )
+
+    def ret_copy(s, g):
+        return remote(
+            ret.at[s, :, box_lanes(g)],
+            back.at[s, :, box_lanes(g)],
             ret_s,
-            ret_r.at[g],
+            ret_r.at[s, g],
             (ahead, sub),
         )
+
+    def flag_copy():
+        return remote(flag, told, flag_s, flag_r, (ahead, sub))
 
     def mate_copy(k):
         return remote(
@@ -385,6 +389,19 @@
         shift_z.append(corners[1, j] - corners[1, i])
         weight.append(jnp.where(count[0] > s, jnp.float32(1.0), jnp.float32(0.0)))
 
+    pl.semaphore_wait(barrier, 4 + SUBS - 1)
+
+    def send_boxes(g, _):
+        box_copy(g).start()
+        return 0
+
+    lax.fori_loop(0, CHUNKS, send_boxes, 0)
+    for s in range(2):
+        for k in range(2):
+            mark = jnp.where(second[s] == 2 + k, jnp.float32(1.0), jnp.float32(0.0))
+            flag[s, k] = jnp.zeros((8, 128), F32) + mark
+    flag_copy().start()
+
     row, col = iotas(LANES, GLANES)
     at = col - row - 32 * band(row)
     for o in range(2):
@@ -394,14 +411,7 @@
     for o in range(2):
         put_x[:, 2 * o * B : (2 * o + 2) * B] = twice(hot(at == start_x[o]))
 
-    pl.semaphore_wait(barrier, 4 + SUBS - 1)
     load.wait()
-
-    def send_boxes(g, _):
-        box_copy(g).start()
-        return 0
-
-    lax.fori_loop(0, CHUNKS, send_boxes, 0)
     halo_copy(0).start()
     halo_copy(1).start()
 
@@ -427,20 +437,10 @@
     at = col - row
     for s in range(2):
         dz_to[s] = hot(same & (at == shift_z[s]))
-        dz_from[s] = hot(same & (at == -shift_z[s]))
     row, col = iotas(B, B)
     at = row - col
     for s in range(2):
         dx_to[s] = twice(hot(at == shift_x[s]))
-        dx_from[s] = twice(hot(at == -shift_x[s]))
-    row, col = iotas(GLANES, LANES)
-    at = row - col - 32 * band(col)
-    for o in range(2):
-        get_z[o] = hot(at == start_z[o])
-    row, col = iotas(B, REACH * SX)
-    at = col - row
-    for o in range(2):
-        get_x[o * B : (o + 1) * B, :] = twice(hot(at == start_x[o]))
 
     mate_copy(HOPS - 1).wait_recv()
     for c in range(RING):
@@ -489,17 +489,14 @@
             rhos.append(jnp.where(first[s] == 0, boxes[0], boxes[1]) * shifted)
         wides = right3(rhos, wide_h[...], wide_l[...])
         for s in range(2):
-            for k in range(0, GROUP, 2):
-                two = left3(left[...], wides[s][:, k * GZ : (k + 2) * GZ])
-                for m in range(2):
-                    rows = pl.ds(pl.multiple_of((g * GROUP + k + m) * ROWS, 8), ROWS)
-                    for q in range(SUBS):
-                        spec[s, q, rows, :] = two[
-                            q * ROWS : (q + 1) * ROWS, m * GZ : (m + 1) * GZ
-                        ]
-        for k in (2, 1, 3):
-            one_copy(k, g).start()
-        one_own(g).start()
+            both = left3(left[...], wides[s])
+            for m in range(PACK):
+                rows = pl.ds(pl.multiple_of((g * PACK + m) * ROWS, 8), ROWS)
+                for q in range(SUBS):
+                    spec[s, q, rows, :] = both[q * ROWS : (q + 1) * ROWS, m * 128 : (m + 1) * 128]
+            for k in (2, 1, 3):
+                one_copy(k, s, g).start()
+            one_own(s, g).start()
         return 0
 
     lax.fori_loop(0, CHUNKS, forward, 0)
@@ -525,116 +522,109 @@
             fld_copy(j + 1, c).start()
         give_copy(j).start()
 
-    def wait_one(g, _):
+    row, col = iotas(LANES, LANES)
+    same = band(row) == band(col)
+    at = col - row
+    for s in range(2):
+        dz_from[s] = hot(same & (at == -shift_z[s]))
+    row, col = iotas(B, B)
+    at = row - col
+    for s in range(2):
+        dx_from[s] = twice(hot(at == -shift_x[s]))
+    row, col = iotas(GLANES, LANES)
+    at = row - col - 32 * band(col)
+    for o in range(2):
+        get_z[o] = hot(at == start_z[o])
+    row, col = iotas(B, REACH * SX)
+    at = col - row
+    for o in range(2):
+        get_x[o * B : (o + 1) * B, :] = twice(hot(at == start_x[o]))
+    lane = lax.broadcasted_iota(jnp.int32, (ROWS, 128), 1)
+
+    def along_y(s, t):
+        a = 2 * t
+        pieces, values = [], []
+        for m in range(2):
+            level = eigen[sub * ROWS + a + m]
+            pieces.append((4.0 * math.pi) / (level_bc[...] + level))
+            tiles = [
+                pencil[s, pl.ds(k * ROWS + a + m, SUBS * CHUNKS, stride=SLICE), :]
+                for k in range(PACK)
+            ]
+            last = [pltpu.roll(tiles[k], 32 * (k + 1), 1) for k in range(PACK)]
+            rest = jnp.where(lane < 32, last[0], jnp.where(lane < 64, last[1], last[2]))
+            values.append(jnp.concatenate(tiles + [rest], axis=0))
+        factor = jnp.concatenate(pieces, axis=1)
+        value = left3(into[...], jnp.concatenate(values, axis=1))
+        value = left3(outof[...], factor * value)
+        for m in range(2):
+            tile = value[:, m * 128 : (m + 1) * 128]
+            rest = tile[PACK * ROWS :]
+            for k in range(PACK):
+                packed = jnp.where(
+                    lane < B, tile[k * ROWS : (k + 1) * ROWS], pltpu.roll(rest, B - 32 * k, 1)
+                )
+                turned[s, pl.ds(k * ROWS + a + m, SUBS * CHUNKS, stride=SLICE), :] = packed
+
+    def middle(s):
+        def wait_one(g, _):
+            for k in range(1, SUBS):
+                one_copy(k, s, g).wait_recv()
+            one_own(s, g).wait()
+            return 0
+
+        def turn(t, _):
+            along_y(s, t)
+            return 0
+
+        def send_two(g, _):
+            for k in (2, 1, 3):
+                two_copy(k, s, g).start()
+            two_own(s, g).start()
+            return 0
+
+        lax.fori_loop(0, CHUNKS, wait_one, 0)
+        lax.fori_loop(0, ROWS // 2, turn, 0)
+        lax.fori_loop(0, CHUNKS, send_two, 0)
+
+    middle(0)
+    field_step(1)
+    middle(1)
+
+    def inverse(s, g):
         for k in range(1, SUBS):
-            one_copy(k, g).wait_recv()
-        one_own(g).wait()
+            two_copy(k, s, g).wait_recv()
+        two_own(s, g).wait()
+        pieces = []
+        for m in range(PACK):
+            rows = pl.ds(pl.multiple_of((g * PACK + m) * ROWS, 8), ROWS)
+            pieces.append(jnp.concatenate([solved[s, q, rows, :] for q in range(SUBS)], axis=0))
+        spread = left3(left[...], jnp.concatenate(pieces, axis=1))
+        potential = right3([spread], narrow_h[...], narrow_l[...])[0]
+        potential = potential * (weight[s] * FOCK_SHARE)
+        onto_first = potential * moved[s, :, box_lanes(g)]
+        box = jnp.where(first[s] == 0, obx[0, :, own_lanes(g)], obx[1, :, own_lanes(g)])
+        onto_second = dot(dx_from[s], pick1(potential * box, dz_from[s]))
+        ret[s, :, box_lanes(g)] = onto_second
+        ret_copy(s, g).start()
+        for k in range(2):
+            out[k, :, box_lanes(g)] -= jnp.where(first[s] == k, onto_first, 0.0) + jnp.where(
+                second[s] == k, onto_second, 0.0
+            )
+
+    def inverse_first(g, _):
+        inverse(0, g)
+        field_step(2 + g)
         return 0
 
-    lax.fori_loop(0, CHUNKS, wait_one, 0)
-
-    def along_y(e, t):
-        a = 2 * t
-        pieces = []
-        for m in range(2):
-            level = eigen[sub * ROWS + 8 * e + a + m]
-            pieces.append((4.0 * math.pi) / (level_bc[...] + level))
-        factor = jnp.concatenate(pieces, axis=1)
-        for s in range(2):
-            parts = []
-            for m in range(2):
-                parts.append(
-                    jnp.concatenate(
-                        [
-                            pencil[s, q, pl.ds(8 * e + a + m, ROWS, stride=ROWS), :]
-                            for q in range(SUBS)
-                        ],
-                        axis=0,
-                    )
-                )
-            value = jnp.concatenate(parts, axis=1)
-            value = left3(left[...], factor * left3(left[...], value))
-            for m in range(2):
-                for q in range(SUBS):
-                    turned[s, q, e, pl.ds(a + m, ROWS, stride=8), :] = value[
-                        q * ROWS : (q + 1) * ROWS, m * GZ : (m + 1) * GZ
-                    ]
-
-    def octet(e, _):
-        def turn(t, _):
-            along_y(e, t)
-            return 0
-
-        lax.fori_loop(0, 4, turn, 0)
-        two_send(e, None)
-        field_step(1 + e)
+    def inverse_second(g, _):
+        inverse(1, g)
         return 0
 
-    lax.fori_loop(0, OCTS - 1, octet, 0)
-
-    def turn_last(t, _):
-        along_y(OCTS - 1, t)
-        return 0
-
-    lax.fori_loop(0, 4, turn_last, 0)
-
-    def send_two(g, _):
-        two_send(OCTS - 1, g)
-        return 0
-
-    lax.fori_loop(0, CHUNKS, send_two, 0)
-    for e in range(OCTS - 1):
-        two_wait(e, None)
-
-    def inverse(g, _):
-        two_wait(OCTS - 1, g)
-        boxes = [obx[0, :, own_lanes(g)], obx[1, :, own_lanes(g)]]
-        mine = [None, None]
-        theirs = [None, None]
-
-        def add(held, k, value):
-            held[k] = value if held[k] is None else held[k] + value
-
-        wides = []
-        for s in range(2):
-            parts = []
-            for k in range(0, GROUP, 2):
-                pieces = []
-                for m in range(2):
-                    rows = pl.ds(pl.multiple_of((g * GROUP + k + m) * 8, 8), 8)
-                    pieces.append(
-                        jnp.concatenate(
-                            [solved[s, q, e, rows, :] for q in range(SUBS) for e in range(OCTS)],
-                            axis=0,
-                        )
-                    )
-                parts.append(left3(left[...], jnp.concatenate(pieces, axis=1)))
-            wides.append(jnp.concatenate(parts, axis=1))
-        potentials = right3(wides, narrow_h[...], narrow_l[...])
-        for s in range(2):
-            potential = potentials[s] * (weight[s] * FOCK_SHARE)
-            onto_first = potential * moved[s, :, box_lanes(g)]
-            onto_second = dot(
-                dx_from[s],
-                pick1(potential * jnp.where(first[s] == 0, boxes[0], boxes[1]), dz_from[s]),
-            )
-            for k in range(2):
-                add(mine, k, jnp.where(first[s] == k, onto_first, 0.0))
-                add(mine, k, jnp.where(second[s] == k, onto_second, 0.0))
-                add(theirs, k, jnp.where(second[s] == 2 + k, onto_second, 0.0))
-        for k in range(2):
-            out[k, :, box_lanes(g)] -= mine[k]
-            ret[k, :, box_lanes(g)] = theirs[k]
-        ret_copy(g).start()
-        return 0
-
-    def inverse_step(g, _):
-        field_step(OCTS + g)
-        return inverse(g, _)
-
-    lax.fori_loop(0, CHUNKS - 1, inverse_step, 0)
+    lax.fori_loop(0, CHUNKS, inverse_first, 0)
     field_last()
-    inverse(CHUNKS - 1, 0)
+    lax.fori_loop(0, CHUNKS, inverse_second, 0)
+    flag_copy().wait_recv()
 
     def wait_give(j, _):
         give_copy(j).wait_recv()
@@ -645,22 +635,29 @@
     def finish(g, _):
         field = fw[1 : REACH + 1, :, grid_lanes(g)].reshape(REACH * SX, GLANES)
         local = dot(get_x[...], stack(field))
-        ret_copy(g).wait_recv()
+        for s in range(2):
+            ret_copy(s, g).wait_recv()
+        came_back = [back[s, :, box_lanes(g)] for s in range(2)]
         for o in range(2):
             here = right1(local[o * B : (o + 1) * B], get_z[o])
-            out[o, :, box_lanes(g)] += (
-                here * obx[o, :, own_lanes(g)] - back[o, :, box_lanes(g)]
-            )
+            total = here * obx[o, :, own_lanes(g)]
+            for s in range(2):
+                marks = jnp.concatenate([told[s, o]] * (LANES // 128), axis=1)
+                marks = jnp.concatenate([marks] * (B // 8), axis=0)
+                total = total - marks * came_back[s]
+            out[o, :, box_lanes(g)] += total
         return 0
 
     lax.fori_loop(0, CHUNKS, finish, 0)
 
-    remote(obx.at[:, :, EDGE : EDGE + ROWS * B], nxt, box_s, box_r.at[0], (behind, sub)).wait_send()
-    remote(ret, back, ret_s, ret_r.at[0], (ahead, sub)).wait_send()
+    remote(orb, nxt, box_s, box_r.at[0], (behind, sub)).wait_send()
+    remote(ret, back, ret_s, ret_r.at[0, 0], (ahead, sub)).wait_send()
+    flag_copy().wait_send()
     for k in range(1, SUBS):
         who = lax.rem(sub + k, SUBS)
-        remote(spec.at[:, who], pencil.at[:, sub], one_s.at[k - 1], one_r.at[0, 0], (slab, who)).wait_send()
-        remote(turned.at[:, who], solved.at[:, sub], two_s.at[k - 1], two_r.at[0, 0], (slab, who)).wait_send()
+        whole = solved.at[:, 0]
+        remote(whole, whole, one_s.at[k - 1], one_r.at[0, 0, 0], (slab, who)).wait_send()
+        remote(whole, whole, two_s.at[k - 1], two_r.at[0, 0, 0], (slab, who)).wait_send()
     halo_copy(0).wait_send()
     halo_copy(1).wait_send()
     eight = win.at[0:HOPS]
@@ -679,8 +676,8 @@
     eigen = jnp.asarray(table[-1])
     dma = pltpu.SemaphoreType.DMA
     part = (2, B, ROWS * B)
-    turns = (2, SUBS, ROWS * ROWS, GZ)
-    octs = (2, SUBS, OCTS, ROWS * 8, GZ)
+    parted = (2, SUBS, CHUNKS * SLICE, 128)
+    joined = (2, SUBS * CHUNKS * SLICE, 128)
     block = (SX, ROWS * GZ)
     return pl.pallas_call(
         functools.partial(kernel, slabs),
@@ -691,16 +688,18 @@
             pltpu.VMEM((2, B, ROWS * B + 2 * EDGE), F32),
             pltpu.VMEM(part, F32),
             pltpu.VMEM(part, F32),
-            pltpu.VMEM(turns, F32),
-            pltpu.VMEM(turns, F32),
-            pltpu.VMEM(octs, F32),
-            pltpu.VMEM(octs, F32),
+            pltpu.VMEM(parted, F32),
+            pltpu.VMEM(joined, F32),
+            pltpu.VMEM(joined, F32),
+            pltpu.VMEM(parted, F32),
             pltpu.VMEM((REACH + 1,) + block, F32),
             pltpu.VMEM((HOPS + 1,) + block, F32),
             pltpu.VMEM((HOPS,) + block, F32),
             pltpu.VMEM((REACH + 3,) + block, F32),
             pltpu.VMEM(part, F32),
             pltpu.VMEM(part, F32),
+            pltpu.VMEM((2, 2, 8, 128), F32),
+            pltpu.VMEM((2, 2, 8, 128), F32),
             pltpu.VMEM((2, LANES, LANES), BF16),
             pltpu.VMEM((2, LANES, LANES), BF16),
             pltpu.VMEM((2, B, 2 * B), BF16),
@@ -715,13 +714,15 @@
             dma((2,)),
             dma((2,)),
             dma((SUBS - 1,)),
-            dma((SUBS - 1, CHUNKS)),
-            dma((CHUNKS,)),
+            dma((SUBS - 1, 2, CHUNKS)),
+            dma((2, CHUNKS)),
             dma((SUBS - 1,)),
-            dma((SUBS - 1, OCTS - 1 + CHUNKS)),
-            dma((OCTS - 1 + CHUNKS,)),
-            dma,
-            dma((CHUNKS,)),
+            dma((SUBS - 1, 2, CHUNKS)),
+            dma((2, CHUNKS)),
+            dma,
+            dma((2, CHUNKS)),
+            dma,
+            dma,
             dma,
             dma((HOPS,)),
             dma,

time: 106 us -> 97.8 us (0.923)
  Pallas kernels: 102 us -> 93.2 us
    pallas_call x1, Pallas kernels: 102 us -> 93.2 us  [local(): pl.pallas_call(functools.partial(kernel, slabs), out_shape=jax.ShapeDtype...]
where the time goes in v2:
time: 97.8 us; the launch traced here: 96.6 us
  Pallas kernels  93.2 us (95%)
  local copies, waits for them, and re-layouts  2.8 us (3%)
    pallas_call x1, Pallas kernels, local(): pl.pallas_call(functools.partial(kernel, slabs), out_shape=jax.ShapeDtype...  93.2 us
    unnamed x1, local copies, waits for them, and re-layouts  2.8 us

profile of v2, /device:TPU:6, one launch (start us, length us, event | category | flops | bytes accessed | tf_op | source)
XLA Modules:
  0.0 96.6 jit_solution(218117647145310041)
XLA Ops:
  0.7 93.2 %orbitals.1 = f32[2,96,2304]{2,1,0:T(8,128)} custom-call(s32[2,256]{1,0:T(2,128)} %bitcast.1, s32[2,2]{1,0:T(2,128)} %pairs.1, s32[1]{0:T(128)S(6)} %copy.18.count, f32[96]{0:T(128)} %constant.32.clone.eigen, f32[2,96,2304]{2,1,0:T(8,128)} %orb.1, f32[8,3072]{1,0:T(8,128)} %ext.1, bf16[192,192]{1,0:T(8,128)(2,1)} %constant.22.clone.left, ...), custom_call_target="tpu_custom_call" | custom-call | tf_op jit(solution)/shard_map/orbitals/pallas_call | solution.py:682
  93.8 2.8 %copy.19 = f32[2,96,2304]{2,1,0:T(8,128)} copy(f32[2,96,2304]{2,1,0:T(8,128)} %orbitals.1) | data formatting | bytes 3538944

commit v3 on v2

--- a/solution.py
+++ b/solution.py
@@ -424,7 +424,7 @@
         win[0:REACH, :, grid_lanes(g)] = total.reshape(REACH, SX, GLANES)
         return 0
 
-    lax.fori_loop(0, CHUNKS, deposit, 0)
+    lax.fori_loop(0, CHUNKS, deposit, 0, unroll=2)
 
     def send_mate(k, _):
         mate_copy(HOPS - 1 - k).start()
@@ -584,7 +584,7 @@
             return 0
 
         lax.fori_loop(0, CHUNKS, wait_one, 0)
-        lax.fori_loop(0, ROWS // 2, turn, 0)
+        lax.fori_loop(0, ROWS // 2, turn, 0, unroll=2)
         lax.fori_loop(0, CHUNKS, send_two, 0)
 
     middle(0)
@@ -612,18 +612,22 @@
                 second[s] == k, onto_second, 0.0
             )
 
-    def inverse_first(g, _):
-        inverse(0, g)
-        field_step(2 + g)
-        return 0
-
-    def inverse_second(g, _):
-        inverse(1, g)
-        return 0
-
-    lax.fori_loop(0, CHUNKS, inverse_first, 0)
+    field_step(2)
+
+    def two_chunks(s, first_step):
+        def body(p, _):
+            field_step(first_step + p)
+            inverse(s, 2 * p)
+            inverse(s, 2 * p + 1)
+            return 0
+
+        return body
+
+    lax.fori_loop(0, CHUNKS // 2, two_chunks(0, 3), 0)
+    lax.fori_loop(0, CHUNKS // 2 - 1, two_chunks(1, 3 + CHUNKS // 2), 0)
     field_last()
-    lax.fori_loop(0, CHUNKS, inverse_second, 0)
+    inverse(1, CHUNKS - 2)
+    inverse(1, CHUNKS - 1)
     flag_copy().wait_recv()
 
     def wait_give(j, _):
@@ -648,7 +652,7 @@
             out[o, :, box_lanes(g)] += total
         return 0
 
-    lax.fori_loop(0, CHUNKS, finish, 0)
+    lax.fori_loop(0, CHUNKS, finish, 0, unroll=2)
 
     remote(orb, nxt, box_s, box_r.at[0], (behind, sub)).wait_send()
     remote(ret, back, ret_s, ret_r.at[0, 0], (ahead, sub)).wait_send()

time: 97.8 us -> 87.4 us (0.89); the launches traced: 96.6 us -> 87.2 us
  Pallas kernels: 93.2 us -> 83.8 us
    pallas_call x1, Pallas kernels: 93.2 us -> 83.8 us  [local(): pl.pallas_call(functools.partial(kernel, slabs), out_shape=jax.ShapeDtype...]
where the time goes in v3:
time: 87.4 us; the launch traced here: 87.2 us
  Pallas kernels  83.8 us (96%)
  local copies, waits for them, and re-layouts  2.8 us (3%)
    pallas_call x1, Pallas kernels, local(): pl.pallas_call(functools.partial(kernel, slabs), out_shape=jax.ShapeDtype...  83.8 us
    unnamed x1, local copies, waits for them, and re-layouts  2.8 us

profile of v3, /device:TPU:6, one launch (start us, length us, event | category | flops | bytes accessed | tf_op | source)
XLA Modules:
  0.0 87.2 jit_solution(12668356195271284877)
XLA Ops:
  0.7 83.8 %orbitals.1 = f32[2,96,2304]{2,1,0:T(8,128)} custom-call(s32[2,256]{1,0:T(2,128)} %bitcast.1, s32[2,2]{1,0:T(2,128)} %pairs.1, s32[1]{0:T(128)S(6)} %copy.18.count, f32[96]{0:T(128)} %constant.32.clone.eigen, f32[2,96,2304]{2,1,0:T(8,128)} %orb.1, f32[8,3072]{1,0:T(8,128)} %ext.1, bf16[192,192]{1,0:T(8,128)(2,1)} %constant.22.clone.left, ...), custom_call_target="tpu_custom_call" | custom-call | tf_op jit(solution)/shard_map/orbitals/pallas_call | solution.py:686
  84.4 2.8 %copy.19 = f32[2,96,2304]{2,1,0:T(8,128)} copy(f32[2,96,2304]{2,1,0:T(8,128)} %orbitals.1) | data formatting | bytes 3538944
